TPU v7x, 128 devices: a whole 4x4x4 slice. The times are simulated.
128 devices in a mesh: dp: 128 (over x, y, z, core).
Axes of the slice: x: 4, y: 4, z: 4, core: 2. Of those that a mesh axis runs over, the one named last changes fastest.
Arguments:
- hidden_in: bfloat16 [131072, 1024], P('dp'), may hold values from -15 to 15
- lengths: int32 [128, 8], P('dp'), may hold values from 1 to 512, 1024 in all within a row
- owner: int32 [1024], P('dp'), may hold values from 0 to 1023, each once
- pooled_grad: float32 [1024, 1024], P('dp'), may hold values from -6 to 6
- norm_gain: bfloat16 [1024], replicated, may hold values from 0.25 to 1.75
- w_query: bfloat16 [1024, 2048], replicated
- w_key: bfloat16 [1024, 1024], P('dp')
- value_weight: bfloat16 [1024, 1024], P('dp'), may hold values from -0.1875 to 0.1875
- w_out: bfloat16 [2048, 1024], replicated, may hold values from -0.125 to 0.125
Outputs:
- grad_in: bfloat16 [131072, 1024], P('dp')
- grad_key: float32 [1024, 1024], P('dp')
- grad_value: float32 [1024, 1024], P('dp')
- grad_gain: float32 [1024], replicated
Inputs may be any that keep to these rules, and one draw needn't show every extreme that they name: Each row of lengths sums to 1024, and some statement has exactly 512 tokens. `owner`: a permutation.
All inputs are finite; a program needn't handle non-finite values.
Results may differ from a plain program's by a relative error of at most 0.035.
The roundings to bfloat16 on the way count: a program that leaves them out, or rounds other values in their place, can miss the bound.
Values may be sent and summed in bfloat16 or wider, within the bound.
A program may use at most 128 MiB of HBM per device.

v0:
```python
import jax
import jax.numpy as jnp
from jax import lax
from jax.sharding import PartitionSpec as P

QUERY_HEADS = 16
KEY_HEADS = 8
HEAD_WIDTH = 128


def per_device(
    hidden_in, lengths, owner, pooled_grad, norm_gain, w_query, w_key, value_weight, w_out
):
    token_rows = hidden_in.shape[0]
    statement_slots = lengths.shape[1]
    key_value_width = w_key.shape[1]
    head_groups = QUERY_HEADS // KEY_HEADS
    scale_q = 1.0 / HEAD_WIDTH**0.5
    every_grad = lax.all_gather(pooled_grad.astype(jnp.bfloat16), "dp", axis=0, tiled=True).astype(
        pooled_grad.dtype
    )
    cached = jnp.take(every_grad, owner, axis=0)
    inputs_f = hidden_in.astype(jnp.float32)
    inv_rms = lax.rsqrt(jnp.mean(inputs_f * inputs_f, axis=-1, keepdims=True) + 1e-06)
    normed = inputs_f * inv_rms
    normed_b = (normed * norm_gain.astype(jnp.float32)).astype(jnp.bfloat16)
    kv_rows = jnp.concatenate([w_key, value_weight], axis=1)
    kv_full = lax.all_gather(kv_rows, "dp", axis=0, tiled=True)
    key_value_joint = jnp.dot(normed_b, kv_full, preferred_element_type=jnp.float32)
    key_value_joint = key_value_joint.astype(jnp.bfloat16)
    key_rows = key_value_joint[:, :key_value_width].reshape(token_rows, KEY_HEADS, HEAD_WIDTH)
    value_rows = key_value_joint[:, key_value_width:].reshape(token_rows, KEY_HEADS, HEAD_WIDTH)
    ends = jnp.cumsum(lengths[0])
    last_rows = ends - 1
    positions = jnp.arange(token_rows, dtype=jnp.int32)
    segment = jnp.sum((positions[:, None] >= ends[None, :]).astype(jnp.int32), axis=1)
    member = segment[None, :] == jnp.arange(statement_slots, dtype=jnp.int32)[:, None]
    last_normed = jnp.take(normed_b, last_rows, axis=0)
    query_rows = jnp.dot(last_normed, w_query, preferred_element_type=jnp.float32).astype(
        jnp.bfloat16
    )
    query_rows = query_rows.reshape(statement_slots, KEY_HEADS, head_groups, HEAD_WIDTH)
    scores = (
        jnp.einsum("sgqe,tge->sgqt", query_rows, key_rows, preferred_element_type=jnp.float32)
        * scale_q
    )
    scores = jnp.where(member[:, None, None, :], scores, -1e30)
    top = jnp.max(scores, axis=-1, keepdims=True)
    expo = jnp.exp(scores - top)
    probs = expo / jnp.sum(expo, axis=-1, keepdims=True)
    probs_b = probs.astype(jnp.bfloat16)
    attended = jnp.einsum(
        "sgqt,tge->sgqe", probs_b, value_rows, preferred_element_type=jnp.float32
    ).astype(jnp.bfloat16)
    attended = attended.reshape(statement_slots, QUERY_HEADS * HEAD_WIDTH)
    pooled = jnp.take(inputs_f, last_rows, axis=0) + jnp.dot(
        attended, w_out, preferred_element_type=jnp.float32
    )
    inv_len = lax.rsqrt(jnp.sum(pooled * pooled, axis=-1, keepdims=True) + 1e-06)
    embed = pooled * inv_len
    grad_pool = inv_len * (cached - embed * jnp.sum(embed * cached, axis=-1, keepdims=True))
    grad_pool_b = grad_pool.astype(jnp.bfloat16)
    attention_gradient = lax.dot_general(
        grad_pool_b, w_out, (((1,), (1,)), ((), ())), preferred_element_type=jnp.float32
    )
    attention_gradient = attention_gradient.astype(jnp.bfloat16).reshape(
        statement_slots, KEY_HEADS, head_groups, HEAD_WIDTH
    )
    grad_values = jnp.einsum(
        "sgqt,sgqe->tge", probs_b, attention_gradient, preferred_element_type=jnp.float32
    )
    grad_values = grad_values.astype(jnp.bfloat16).reshape(token_rows, key_value_width)
    grad_prob = jnp.einsum(
        "sgqe,tge->sgqt", attention_gradient, value_rows, preferred_element_type=jnp.float32
    )
    grad_score = probs * (grad_prob - jnp.sum(probs * grad_prob, axis=-1, keepdims=True)) * scale_q
    grad_score = grad_score.astype(jnp.bfloat16)
    grad_query = jnp.einsum(
        "sgqt,tge->sgqe", grad_score, key_rows, preferred_element_type=jnp.float32
    )
    grad_query = grad_query.astype(jnp.bfloat16).reshape(statement_slots, QUERY_HEADS * HEAD_WIDTH)
    grad_keys = jnp.einsum(
        "sgqt,sgqe->tge", grad_score, query_rows, preferred_element_type=jnp.float32
    )
    grad_keys = grad_keys.astype(jnp.bfloat16).reshape(token_rows, key_value_width)
    grad_both = jnp.concatenate([grad_keys, grad_values], axis=1)
    grad_normed = lax.dot_general(
        grad_both, kv_full, (((1,), (1,)), ((), ())), preferred_element_type=jnp.float32
    )
    query_back = lax.dot_general(
        grad_query, w_query, (((1,), (1,)), ((), ())), preferred_element_type=jnp.float32
    )
    grad_normed = grad_normed.at[last_rows].add(query_back)
    gain_total = lax.psum(jnp.sum(grad_normed * normed, axis=0), "dp")
    scaled = grad_normed * norm_gain.astype(jnp.float32)
    grad_in = inv_rms * (scaled - normed * jnp.mean(scaled * normed, axis=-1, keepdims=True))
    grad_in = grad_in.at[last_rows].add(grad_pool).astype(jnp.bfloat16)
    weight_share = lax.psum_scatter(
        lax.dot_general(
            normed_b, grad_both, (((0,), (0,)), ((), ())), preferred_element_type=jnp.float32
        ),
        "dp",
        scatter_dimension=0,
        tiled=True,
    )
    return (
        grad_in,
        weight_share[:, :key_value_width],
        weight_share[:, key_value_width:],
        gain_total,
    )


def solution(mesh):
    return jax.shard_map(
        per_device,
        mesh=mesh,
        in_specs=(
            P("dp", None),
            P("dp", None),
            P("dp"),
            P("dp", None),
            P(),
            P(),
            P("dp", None),
            P("dp", None),
            P(),
        ),
        out_specs=(P("dp", None), P("dp", None), P("dp", None), P()),
        check_vma=False,
    )
```

profile of v0, /device:TPU:0, one launch (start us, length us, event | category | flops | bytes accessed | tf_op | source)
XLA Modules:
  0.0 839.9 jit_solution(15867571985289667130)
XLA Ops:
  7.2 1.5 convert_element_type.73
  8.8 1.4 pad_maximum_fusion.3
  10.9 4.0 convert_element_type.64
  15.6 1.9 multiply_convert_fusion
  17.5 2.4 gather_fusion
  19.9 2.8 gather_fusion.1
  22.9 2.9 convolution_convert_fusion.2
  25.8 53.7 %all-gather.5.cloned.1.call-done = bf16[1024,1024]{1,0:T(8,128)(2,1)} async-done(((bf16[8,1024]{1,0:T(8,128)(2,1)}), bf16[1024,1024]{1,0:T(8,128)(2,1)}) %all-gather.5.cloned.1.call-update) | async-done | bytes 2097168 | tf_op jit(solution)/shard_map/all_gather | solution.py:19
  79.5 4.0 convert_element_type.74
  83.5 2.8 gather_fusion.2
  86.3 61.3 %all-gather.3.cloned.1.call-done = bf16[1024,2048]{1,0:T(8,128)(2,1)} async-done(((bf16[8,2048]{1,0:T(8,128)(2,1)}), bf16[1024,2048]{1,0:T(8,128)(2,1)}) %all-gather.3.cloned.1.call-update) | async-done | bytes 4194320 | tf_op jit(solution)/shard_map/all_gather | solution.py:28
  147.6 7.3 convolution_convert_fusion
  154.9 1.2 slice_bitcast_fusion.1
  156.1 2.0 copy.35
  158.1 2.0 copy.36
  160.1 2.4 fusion.58
  162.5 2.3 fusion.33
  166.3 1.2 convolution_convert_fusion.1
  168.2 2.1 bitcast_convert_fusion
  170.3 2.8 bitcast_convert_fusion.1
  173.1 10.6 %fusion.2 = f32[1024,2048]{1,0:T(8,128)} fusion(bf16[1024,1024]{1,0:T(8,128)(2,1)} %multiply_convert_fusion, bf16[1024,1024]{0,1:T(8,128)(2,1)} %bitcast.63, bf16[1024,1024]{0,1:T(8,128)(2,1)} %bitcast.75), kind=kOutput, calls=%fused_computation.16 | convolution fusion | flops 4303355904 | bytes 14680064 | tf_op jit(solution)/shard_map/dot_general | solution.py:99
  183.7 2.4 fusion.30
  186.1 3.5 fusion.61
  189.6 8.4 %fusion.3 = f32[1024,1024]{1,0:T(8,128)} fusion(bf16[1024,2048]{1,0:T(8,128)(2,1)} %all-gather.3.cloned.1.call-done, bf16[1024,1024]{0,1:T(8,128)(2,1)S(1)} %bitcast.64, bf16[1024,1024]{0,1:T(8,128)(2,1)S(1)} %bitcast.76), kind=kOutput, calls=%fused_computation.17 | convolution fusion | flops 4303355904 | bytes 12582912 | tf_op jit(solution)/shard_map/dot_general | solution.py:87
  198.1 4.8 scatter_fusion
  202.8 3.5 multiply_reduce_fusion
  206.3 2.9 subtract_multiply_fusion
  209.3 4.9 scatter_custom_fusion.1
  214.1 3.8 convert_element_type.84
  218.0 64.0 %psum.7 = f32[1024]{0:T(1024)} all-reduce(f32[1024]{0:T(1024)S(1)} %get-tuple-element.5), channel_id=1, replica_groups=mesh['dp'=128] {'dp'}, use_global_device_ids=true, to_apply=%region_13.15 | all-reduce | flops 1024 | bytes 8192 | tf_op jit(solution)/shard_map/psum | solution.py:94
  282.0 550.0 %reduce-scatter.2.cloned.1.call-done = f32[8,2048]{1,0:T(8,128)} async-done(((f32[1024,2048]{1,0:T(8,128)}), f32[8,2048]{1,0:T(8,128)}) %reduce-scatter.2.cloned.1.call-update) | async-done | bytes 65552 | tf_op jit(solution)/shard_map/reduce_scatter | solution.py:98
  831.9 1.4 fusion.57
  (40 shorter events, 3.9 us)
Async XLA Ops:
  7.2 7.9 copy-start
  7.2 7.7 copy-start.5
  7.2 72.3 %all-gather.5.cloned.1.call-start = ((), (), s32[]{:S(2)}) async-start(), calls=%async_computation.2 | async-start | bytes 2113536 | tf_op jit(solution)/shard_map/all_gather | solution.py:19
  8.8 138.8 %all-gather.3.cloned.1.call-start = ((), (), s32[]{:S(2)}) async-start(), calls=%async_computation.1 | async-start | bytes 4227072 | tf_op jit(solution)/shard_map/all_gather | solution.py:28
  10.2 821.8 %reduce-scatter.2.cloned.1.call-start = ((), (), s32[]{:S(2)}) async-start(), calls=%async_computation.3 | async-start | bytes 8454144 | tf_op jit(solution)/shard_map/reduce_scatter | solution.py:98
  14.9 7.8 copy-start.6
  162.5 2.8 copy-start.2
  165.3 2.2 copy-start.4
  186.1 3.5 copy-start.3
  186.1 3.5 copy-start.7
  202.8 3.5 copy-start.1
Sparse Core Ops, SparseCore 0:
  11.7 67.7 all-gather.4
  83.2 64.2 all-gather.2
  183.8 648.0 reduce-scatter.1
where the time goes:
time: 841 us; the launch traced here: 840 us
  waiting for transfers between devices  665 us (79%)
  blocking collectives  64 us (8%)
  matrix products  47.4 us (6%)
  other arithmetic  34.3 us (4%)
  local copies, waits for them, and re-layouts  15.1 us (2%)
  between operations  13.9 us (2%)
    reduce_scatter x1, waiting for transfers between devices, per_device(): lax.psum_scatter(lax.dot_general(normed_b, grad_both, (((0,), (0,)), ((),...  550 us
    psum x1, blocking collectives, per_device(): gain_total = lax.psum(jnp.sum(grad_normed * normed, axis=0), 'dp')  64 us
    all_gather x1, waiting for transfers between devices, per_device(): kv_full = lax.all_gather(kv_rows, 'dp', axis=0, tiled=True)  61.3 us
    all_gather x1, waiting for transfers between devices, per_device(): lax.all_gather(pooled_grad.astype(jnp.bfloat16), 'dp', axis=0, tiled=True)  53.7 us
  transfers between devices with their start and end apart: 3, of which 3 were waited for; matrix products, arithmetic and copies ran while one was open for 7% of the time, Pallas kernels for 0%

commit v1 on v0

--- a/solution.py
+++ b/solution.py
@@ -1,11 +1,305 @@
+import functools
 import jax
 import jax.numpy as jnp
 from jax import lax
+from jax.experimental import pallas as pl
+from jax.experimental.pallas import tpu as pltpu
 from jax.sharding import PartitionSpec as P
 
 QUERY_HEADS = 16
 KEY_HEADS = 8
 HEAD_WIDTH = 128
+RING = 4
+STRIDES = (32, 8, 2)
+ORDERS = ((0, 1, 2), (1, 2, 0), (2, 0, 1))
+MESH = pl.DeviceIdType.MESH
+
+
+def place():
+    me = lax.axis_index("dp")
+    return me, ((me // 32) % 4, (me // 8) % 4, (me // 2) % 4), me % 2
+
+
+def peer_of(me, coords, dim, delta):
+    there = (coords[dim] + delta) % RING
+    return there, me + (there - coords[dim]) * STRIDES[dim]
+
+
+def greet(me, coords, core):
+    barrier = pltpu.get_barrier_semaphore()
+    pl.semaphore_signal(barrier, inc=1, device_id=(me + 1 - 2 * core,), device_id_type=MESH)
+    for dim in range(3):
+        for delta in range(1, RING):
+            _, other = peer_of(me, coords, dim, delta)
+            pl.semaphore_signal(barrier, inc=1, device_id=(other,), device_id_type=MESH)
+    pl.semaphore_wait(barrier, 10)
+
+
+def send(src, dst, sems, where, other):
+    copy = pltpu.make_async_remote_copy(
+        src_ref=src,
+        dst_ref=dst,
+        send_sem=sems.at[(0,) + where],
+        recv_sem=sems.at[(1,) + where],
+        device_id=(other,),
+        device_id_type=MESH,
+    )
+    copy.start()
+    return copy
+
+
+def slab(ref, coords, core, dims):
+    index = [coords[0], coords[1], coords[2], core]
+    for dim in dims:
+        index[dim] = slice(None)
+    return ref.at[tuple(index)]
+
+
+def gather_kernel(key_ref, value_ref, grad_ref, kv_out, grad_out, sems, pair_sems, own_sems):
+    me, coords, core = place()
+    sibling = me + 1 - 2 * core
+    width = key_ref.shape[1]
+    sources = (key_ref, value_ref, grad_ref)
+    targets = (
+        kv_out.at[:, :, :, :, :, pl.ds(0, width)],
+        kv_out.at[:, :, :, :, :, pl.ds(width, width)],
+        grad_out,
+    )
+    own = []
+    for part in range(3):
+        copy = pltpu.make_async_copy(
+            sources[part], slab(targets[part], coords, core, ()), own_sems.at[part]
+        )
+        copy.start()
+        own.append(copy)
+    greet(me, coords, core)
+    stages = [[], [], []]
+    for part in range(3):
+        dim = ORDERS[part][0]
+        for delta in range(1, RING):
+            _, other = peer_of(me, coords, dim, delta)
+            stages[part].append(
+                send(
+                    sources[part],
+                    slab(targets[part], coords, core, ()),
+                    sems,
+                    (part, 0, delta - 1),
+                    other,
+                )
+            )
+    last = [[], [], []]
+    for step in (1, 2):
+        for part in range(3):
+            if step == 1:
+                own[part].wait()
+            for copy in stages[part]:
+                copy.wait()
+            stages[part] = []
+            done = ORDERS[part][:step]
+            dim = ORDERS[part][step]
+            piece = slab(targets[part], coords, core, done)
+            for delta in (2, 1, 3):
+                _, other = peer_of(me, coords, dim, delta)
+                stages[part].append(send(piece, piece, sems, (part, step, delta - 1), other))
+            if step == 2:
+                last[part].append(send(piece, piece, pair_sems, (part, 0), sibling))
+    for part in range(3):
+        dim = ORDERS[part][2]
+        done = ORDERS[part][:2]
+        for at, delta in ((1, 1), (2, 3), (0, 2)):
+            stages[part][at].wait()
+            there = list(coords)
+            there[dim] = (coords[dim] + RING - delta) % RING
+            piece = slab(targets[part], there, core, done)
+            last[part].append(send(piece, piece, pair_sems, (part, delta), sibling))
+    for part in range(3):
+        for copy in last[part]:
+            copy.wait()
+
+
+def gather_all(key_rows, value_rows, grad_rows):
+    rows, width = key_rows.shape
+    grid = (RING, RING, RING, 2, rows)
+    kv, grads = pl.pallas_call(
+        gather_kernel,
+        out_shape=(
+            jax.ShapeDtypeStruct(grid + (2 * width,), jnp.bfloat16),
+            jax.ShapeDtypeStruct(grid + (width,), jnp.bfloat16),
+        ),
+        in_specs=[pl.BlockSpec(memory_space=pltpu.VMEM)] * 3,
+        out_specs=(
+            pl.BlockSpec(memory_space=pltpu.VMEM),
+            pl.BlockSpec(memory_space=pltpu.VMEM),
+        ),
+        scratch_shapes=[
+            pltpu.SemaphoreType.DMA((2, 3, 3, 3)),
+            pltpu.SemaphoreType.DMA((2, 3, 4)),
+            pltpu.SemaphoreType.DMA((3,)),
+        ],
+        compiler_params=pltpu.CompilerParams(
+            collective_id=0, has_side_effects=True, vmem_limit_bytes=40 * 2**20
+        ),
+        name="gather_rows",
+    )(key_rows, value_rows, grad_rows)
+    total = 2 * RING**3 * rows
+    return kv.reshape(total, 2 * width), grads.reshape(total, width)
+
+
+def f32(value):
+    return value.astype(jnp.float32)
+
+
+def scatter_kernel(cuts, share_ref, gain_ref, out_ref, gain_out, *scratch):
+    pair_in, first, first_in, second, second_in, third, third_in = (
+        scratch[3 * i : 3 * i + 3] for i in range(7)
+    )
+    gain_pair, gain_sum, gain_in, sems, pair_sems, gain_sems, gain_pair_sem = scratch[21:]
+    me, coords, core = place()
+    sibling = me + 1 - 2 * core
+    greet(me, coords, core)
+    gain_copy = send(gain_ref, gain_pair, gain_pair_sem, (0,), sibling)
+    pairs = []
+    for part, (low, size) in enumerate(cuts):
+        pairs.append(
+            send(
+                share_ref.at[:, :, :, 1 - core, :, pl.ds(low, size)],
+                pair_in[part],
+                pair_sems,
+                (part,),
+                sibling,
+            )
+        )
+
+    def gain_round(dim, value):
+        gain_sum[dim] = value
+        gain_in[dim, coords[dim]] = value
+        copies = []
+        for delta in range(1, RING):
+            _, other = peer_of(me, coords, dim, delta)
+            copies.append(
+                send(
+                    gain_sum.at[dim],
+                    gain_in.at[dim, coords[dim]],
+                    gain_sems,
+                    (dim, delta - 1),
+                    other,
+                )
+            )
+        return copies
+
+    def gain_total(dim, copies):
+        for copy in copies:
+            copy.wait()
+        return (gain_in[dim, 0] + gain_in[dim, 1]) + (gain_in[dim, 2] + gain_in[dim, 3])
+
+    def push(part, step, source, target):
+        copies = []
+        for delta in (2, 1, 3):
+            there, other = peer_of(me, coords, ORDERS[part][step], delta)
+            copies.append(
+                send(source.at[there], target.at[delta - 1], sems, (part, step, delta - 1), other)
+            )
+        return copies
+
+    gain_copy.wait()
+    gain_copies = gain_round(0, gain_ref[...] + gain_pair[...])
+    flights = []
+    for part, (low, size) in enumerate(cuts):
+        pairs[part].wait()
+        order = ORDERS[part]
+
+        @pl.loop(0, RING * RING)
+        def _(at):
+            ahead = [at // RING, at % RING, 0]
+            for z in range(RING):
+                ahead[2] = z
+                value = f32(share_ref[ahead[0], ahead[1], z, core, :, pl.ds(low, size)])
+                value = value + f32(pair_in[part][ahead[0], ahead[1], z])
+                first[part][ahead[order[0]], ahead[order[1]], ahead[order[2]]] = value.astype(
+                    jnp.bfloat16
+                )
+
+        flights.append(push(part, 0, first[part], first_in[part]))
+    gain_copies = gain_round(1, gain_total(0, gain_copies))
+    for part in range(3):
+        for copy in flights[part]:
+            copy.wait()
+        mine = coords[ORDERS[part][0]]
+
+        @pl.loop(0, RING)
+        def _(a):
+            for b in range(RING):
+                value = f32(first[part][mine, a, b]) + f32(first_in[part][0, a, b])
+                value = value + (f32(first_in[part][1, a, b]) + f32(first_in[part][2, a, b]))
+                second[part][a, b] = value.astype(jnp.bfloat16)
+
+        flights[part] = push(part, 1, second[part], second_in[part])
+    gain_copies = gain_round(2, gain_total(1, gain_copies))
+    for part in range(3):
+        for copy in flights[part]:
+            copy.wait()
+        mine = coords[ORDERS[part][1]]
+        for b in range(RING):
+            value = f32(second[part][mine, b]) + f32(second_in[part][0, b])
+            value = value + (f32(second_in[part][1, b]) + f32(second_in[part][2, b]))
+            third[part][b] = value.astype(jnp.bfloat16)
+        flights[part] = push(part, 2, third[part], third_in[part])
+    gain_out[...] = gain_total(2, gain_copies)
+    for part, (low, size) in enumerate(cuts):
+        for copy in flights[part]:
+            copy.wait()
+        mine = coords[ORDERS[part][2]]
+        value = f32(third[part][mine]) + f32(third_in[part][0])
+        value = value + (f32(third_in[part][1]) + f32(third_in[part][2]))
+        out_ref[:, pl.ds(low, size)] = value
+
+
+def scatter_sum(share, gain):
+    total, width = share.shape
+    rows = total // (2 * RING**3)
+    lanes = width // 128
+    sizes = [128 * ((lanes + 2 - part) // 3) for part in range(3)]
+    cuts, low = [], 0
+    for size in sizes:
+        cuts.append((low, size))
+        low += size
+
+    def scratch(*lead):
+        return [pltpu.VMEM(lead + (rows, size), jnp.bfloat16) for _, size in cuts]
+
+    out, gain_total = pl.pallas_call(
+        functools.partial(scatter_kernel, tuple(cuts)),
+        out_shape=(
+            jax.ShapeDtypeStruct((rows, width), jnp.float32),
+            jax.ShapeDtypeStruct((8, gain.shape[0] // 8), jnp.float32),
+        ),
+        in_specs=[pl.BlockSpec(memory_space=pltpu.VMEM)] * 2,
+        out_specs=(
+            pl.BlockSpec(memory_space=pltpu.VMEM),
+            pl.BlockSpec(memory_space=pltpu.VMEM),
+        ),
+        scratch_shapes=scratch(RING, RING, RING)
+        + scratch(RING, RING, RING)
+        + scratch(RING - 1, RING, RING)
+        + scratch(RING, RING)
+        + scratch(RING - 1, RING)
+        + scratch(RING)
+        + scratch(RING - 1)
+        + [
+            pltpu.VMEM((8, gain.shape[0] // 8), jnp.float32),
+            pltpu.VMEM((3, 8, gain.shape[0] // 8), jnp.float32),
+            pltpu.VMEM((3, RING, 8, gain.shape[0] // 8), jnp.float32),
+            pltpu.SemaphoreType.DMA((2, 3, 3, 3)),
+            pltpu.SemaphoreType.DMA((2, 3)),
+            pltpu.SemaphoreType.DMA((2, 3, 3)),
+            pltpu.SemaphoreType.DMA((2, 1)),
+        ],
+        compiler_params=pltpu.CompilerParams(
+            collective_id=1, has_side_effects=True, vmem_limit_bytes=40 * 2**20
+        ),
+        name="scatter_sum",
+    )(share.reshape(RING, RING, RING, 2, rows, width), gain.reshape(8, -1))
+    return out, gain_total.reshape(-1)
 
 
 def per_device(
@@ -16,16 +310,12 @@
     key_value_width = w_key.shape[1]
     head_groups = QUERY_HEADS // KEY_HEADS
     scale_q = 1.0 / HEAD_WIDTH**0.5
-    every_grad = lax.all_gather(pooled_grad.astype(jnp.bfloat16), "dp", axis=0, tiled=True).astype(
-        pooled_grad.dtype
-    )
-    cached = jnp.take(every_grad, owner, axis=0)
+    kv_full, every_grad = gather_all(w_key, value_weight, pooled_grad.astype(jnp.bfloat16))
+    cached = jnp.take(every_grad, owner, axis=0).astype(jnp.float32)
     inputs_f = hidden_in.astype(jnp.float32)
     inv_rms = lax.rsqrt(jnp.mean(inputs_f * inputs_f, axis=-1, keepdims=True) + 1e-06)
     normed = inputs_f * inv_rms
     normed_b = (normed * norm_gain.astype(jnp.float32)).astype(jnp.bfloat16)
-    kv_rows = jnp.concatenate([w_key, value_weight], axis=1)
-    kv_full = lax.all_gather(kv_rows, "dp", axis=0, tiled=True)
     key_value_joint = jnp.dot(normed_b, kv_full, preferred_element_type=jnp.float32)
     key_value_joint = key_value_joint.astype(jnp.bfloat16)
     key_rows = key_value_joint[:, :key_value_width].reshape(token_rows, KEY_HEADS, HEAD_WIDTH)
@@ -91,18 +381,14 @@
         grad_query, w_query, (((1,), (1,)), ((), ())), preferred_element_type=jnp.float32
     )
     grad_normed = grad_normed.at[last_rows].add(query_back)
-    gain_total = lax.psum(jnp.sum(grad_normed * normed, axis=0), "dp")
+    gain_part = jnp.sum(grad_normed * normed, axis=0)
     scaled = grad_normed * norm_gain.astype(jnp.float32)
     grad_in = inv_rms * (scaled - normed * jnp.mean(scaled * normed, axis=-1, keepdims=True))
     grad_in = grad_in.at[last_rows].add(grad_pool).astype(jnp.bfloat16)
-    weight_share = lax.psum_scatter(
-        lax.dot_general(
-            normed_b, grad_both, (((0,), (0,)), ((), ())), preferred_element_type=jnp.float32
-        ),
-        "dp",
-        scatter_dimension=0,
-        tiled=True,
-    )
+    share = lax.dot_general(
+        normed_b, grad_both, (((0,), (0,)), ((), ())), preferred_element_type=jnp.float32
+    ).astype(jnp.bfloat16)
+    weight_share, gain_total = scatter_sum(share, gain_part)
     return (
         grad_in,
         weight_share[:, :key_value_width],

time: 841 us -> 142 us (0.17)
  waiting for transfers between devices: 665 us -> 0 us
  blocking collectives: 64 us -> 0 us
  Pallas kernels: 0 us -> 56 us
  between operations: 13.9 us -> 0.81 us
  matrix products: 47.4 us -> 38.4 us
    reduce_scatter x1 -> x0, waiting for transfers between devices: 550 us -> none  [per_device(): lax.psum_scatter(lax.dot_general(normed_b, grad_both, (((0,), (0,)), ((),...]
    all_gather x2 -> x0, waiting for transfers between devices: 115 us -> none  [the longest x1 61.3 us: per_device(): kv_full = lax.all_gather(kv_rows, 'dp', axis=0, tiled=True)]
    psum x1 -> x0, blocking collectives: 64 us -> none  [per_device(): gain_total = lax.psum(jnp.sum(grad_normed * normed, axis=0), 'dp')]
    pallas_call x0 -> x2, Pallas kernels: none -> 56 us  [the longest x1 31.7 us: gather_all(): pl.pallas_call(gather_kernel, out_shape=(jax.ShapeDtypeStruct(grid + (2 *...]
  transfers between devices with their start and end apart: 3 -> 0, of which waited for: 3 -> 0; matrix products, arithmetic and copies ran while one was open for 7% -> 0% of each run, Pallas kernels for 0% -> 0%
where the time goes in v1:
time: 142 us; the launch traced here: 141 us
  Pallas kernels  56 us (39%)
  matrix products  38.4 us (27%)
  other arithmetic  31.7 us (22%)
  local copies, waits for them, and re-layouts  14.1 us (10%)
    pallas_call x1, Pallas kernels, gather_all(): pl.pallas_call(gather_kernel, out_shape=(jax.ShapeDtypeStruct(grid + (2 *...  31.7 us
    pallas_call x1, Pallas kernels, scatter_sum(): pl.pallas_call(functools.partial(scatter_kernel, tuple(cuts)), out_shape=...  24.3 us
    dot_general x1, matrix products, per_device(): lax.dot_general(grad_both, kv_full, (((1,), (1,)), ((), ())), preferred_e...  8.5 us
    dot_general x1, matrix products, per_device(): lax.dot_general(normed_b, grad_both, (((0,), (0,)), ((), ())), preferred_...  7.86 us
    unnamed x26, local copies, waits for them, and re-layouts  7.73 us
    dot_general x1, matrix products, per_device(): jnp.dot(normed_b, kv_full, preferred_element_type=jnp.float32)  7.32 us
    scatter-add x1, other arithmetic, per_device(): grad_in = grad_in.at[last_rows].add(grad_pool).astype(jnp.bfloat16)  4.79 us
    scatter-add x1, other arithmetic, per_device(): grad_normed = grad_normed.at[last_rows].add(query_back)  4.76 us

profile of v1, /device:TPU:0, one launch (start us, length us, event | category | flops | bytes accessed | tf_op | source)
XLA Modules:
  0.0 141.0 jit_solution(1724769200832671148)
XLA Ops:
  0.6 0.8 reduce-window.4
  1.5 0.7 compare_and_fusion
  2.8 0.7 convert_element_type.68
  3.6 2.1 %multiply_reduce_fusion.2 = f32[1024]{0:T(1024)S(1)} fusion(bf16[1024,1024]{1,0:T(8,128)(2,1)} %param.11), kind=kLoop, calls=%fused_computation.14 | loop fusion | flops 3144704 | bytes 2101248 | tf_op jit(solution)/shard_map/reduce_sum | solution.py:316
  5.7 0.8 convert_element_type.72.grad_ref
  6.5 3.6 %multiply_convert_fusion = bf16[1024,1024]{1,0:T(8,128)(2,1)} fusion(bf16[1024,1024]{1,0:T(8,128)(2,1)} %param.11, f32[1024]{0:T(1024)S(1)} %convert_element_type.68, f32[1024]{0:T(1024)S(1)} %add_rsqrt_fusion), kind=kLoop, calls=%fused_computation.13 | loop fusion | flops 4194304 | bytes 4202496 | tf_op jit(solution)/shard_map/convert_element_type | solution.py:318
  10.1 2.4 %gather_fusion.1 = bf16[8,1024]{1,0:T(8,128)(2,1)S(1)} fusion(bf16[1024,1024]{1,0:T(8,128)(2,1)} %multiply_convert_fusion, s32[1024]{0:T(1024)S(1)} %pad_clamp_fusion.2), kind=kCustom, calls=%fused_computation.clone | custom fusion | bytes 32800 | tf_op jit(solution)/shard_map/jit(_take)/gather | solution.py:328
  12.5 2.9 %convolution_convert_fusion.3 = bf16[8,2048]{1,0:T(8,128)(2,1)S(1)} fusion(bf16[1024,2048]{1,0:T(8,128)(2,1)} %param.16, bf16[8,1024]{1,0:T(8,128)(2,1)S(1)} %gather_fusion.1, pred[8]{0:T(512)(128)(4,1)S(1)} %get-tuple-element.15), kind=kOutput, calls=%fused_computation.19 | convolution fusion | flops 33579008 | bytes 4243464 | tf_op jit(solution)/shard_map/dot_general | solution.py:329
  15.4 2.4 %convert_element_type.67 = f32[1024,1024]{1,0:T(8,128)} convert(bf16[1024,1024]{1,0:T(8,128)(2,1)S(1)} %copy-done.4) | non-fusion elementwise | flops 1048576 | bytes 6291456 | tf_op jit(solution)/shard_map/convert_element_type | solution.py:315
  17.8 2.8 %gather_fusion = f32[8,1024]{1,0:T(8,128)S(1)} fusion(f32[1024,1024]{1,0:T(8,128)} %convert_element_type.67, s32[1024]{0:T(1024)S(1)} %pad_clamp_fusion.1), kind=kCustom, calls=%fused_computation.2 | custom fusion | bytes 65568 | tf_op jit(solution)/shard_map/jit(_take)/gather | solution.py:346
  20.6 31.7 %gather_rows.1 = (bf16[4,4,4,2,8,2048]{5,4,3,2,1,0:T(8,128)(2,1)S(1)}, bf16[4,4,4,2,8,1024]{5,4,3,2,1,0:T(8,128)(2,1)S(1)}) custom-call(bf16[8,1024]{1,0:T(8,128)(2,1)S(1)} %copy-done.1, bf16[8,1024]{1,0:T(8,128)(2,1)S(1)} %copy-done.2, bf16[8,1024]{1,0:T(8,128)(2,1)S(1)} %convert_element_type.72.grad_ref), custom_call_target="tpu_custom_call" | custom-call | tf_op jit(solution)/shard_map/gather_rows/pallas_call | solution.py:123
  52.3 1.9 %copy-done.3 = bf16[4,4,4,2,8,2048]{5,4,3,2,1,0:T(8,128)(2,1)} copy-done((bf16[4,4,4,2,8,2048]{5,4,3,2,1,0:T(8,128)(2,1)}, bf16[4,4,4,2,8,2048]{5,4,3,2,1,0:T(8,128)(2,1)S(1)}, u32[]{:S(2)}) %copy-start.3) | copy-done | bytes 4194328
  54.8 7.3 %convolution_convert_fusion.1 = bf16[1024,2048]{1,0:T(8,128)(2,1)S(1)} fusion(bf16[1024,1024]{1,0:T(8,128)(2,1)} %multiply_convert_fusion, bf16[1024,2048]{1,0:T(8,128)(2,1)} %bitcast.70), kind=kOutput, calls=%fused_computation.16 | convolution fusion | flops 4297064448 | bytes 10485760 | tf_op jit(solution)/shard_map/dot_general | solution.py:319
  62.2 1.0 slice_bitcast_fusion.1
  63.1 2.0 %copy.35 = bf16[128,8,8,128]{3,2,1,0:T(8,128)(2,1)} copy(bf16[128,8,8,128]{3,1,2,0:T(8,128)(2,1)S(1)} %get-tuple-element.17) | data formatting | bytes 4194304
  65.1 2.4 %fusion.65 = (f32[8,8,2]{0,2,1:T(2,128)S(1)}, f32[8,8,2,1024]{3,0,2,1:T(8,128)S(1)}) fusion(bf16[8,8,2,128]{3,0,2,1:T(8,128)(2,1)S(1)} %bitcast.80, bf16[1024,8,128,1]{2,1,0,3:T(8,128)(2,1)} %bitcast.72, pred[8,1024]{1,0:T(8,128)(4,1)S(1)} %iota_compare_fusion), kind=kOutput, calls=%fused_computation.91 | convolution fusion | flops 34079744 | bytes 2662912 | tf_op jit(solution)/shard_map/sub | solution.py:339
  68.7 1.0 copy-done.7
  69.7 0.8 multiply_reduce_fusion.4
  70.7 1.2 convolution_convert_fusion.2
  71.9 0.7 fusion.12
  72.6 0.8 fusion.29
  73.4 3.4 %fusion.68 = f32[8,1024]{1,0:T(8,128)S(1)} fusion(bf16[8,2048]{1,0:T(8,128)(2,1)S(1)} %bitcast.83, bf16[1024,2048]{1,0:T(8,128)(2,1)} %param.16), kind=kOutput, calls=%fused_computation.92 | convolution fusion | flops 33554432 | bytes 4259840 | tf_op jit(solution)/shard_map/dot_general | solution.py:380
  76.8 1.2 bitcast_convert_fusion.1
  78.0 0.8 bitcast_convert_fusion
  79.4 8.5 %fusion.2 = f32[1024,1024]{1,0:T(8,128)} fusion(bf16[1024,2048]{1,0:T(8,128)(2,1)} %bitcast.71, bf16[1024,1024]{0,1:T(8,128)(2,1)S(1)} %bitcast.76, bf16[1024,1024]{0,1:T(8,128)(2,1)S(1)} %bitcast.86), kind=kOutput, calls=%fused_computation.17 | convolution fusion | flops 4303355904 | bytes 12582912 | tf_op jit(solution)/shard_map/dot_general | solution.py:377
  87.9 7.9 %convolution_convert_fusion = bf16[1024,2048]{1,0:T(8,128)(2,1)} fusion(bf16[1024,1024]{1,0:T(8,128)(2,1)S(1)} %copy-done.8, bf16[1024,1024]{0,1:T(8,128)(2,1)S(1)} %bitcast.77, bf16[1024,1024]{0,1:T(8,128)(2,1)} %bitcast.87), kind=kOutput, calls=%fused_computation.15 | convolution fusion | flops 4305453056 | bytes 10485760 | tf_op jit(solution)/shard_map/dot_general | solution.py:388
  95.8 4.8 %scatter_fusion = f32[1024,1024]{1,0:T(8,128)} fusion(f32[1024,1024]{1,0:T(8,128)} %fusion.2, s32[8]{0:T(128)S(1)} %fusion.56, f32[8,1024]{1,0:T(8,128)S(1)} %fusion.68), kind=kCustom, calls=%fused_computation.3 | custom fusion | flops 8192 | bytes 98336 | tf_op jit(solution)/shard_map/scatter-add | solution.py:383
  100.6 3.5 %multiply_reduce_fusion = (f32[1024]{0:T(1024)S(1)}, f32[1024]{0:T(1024)S(1)}) fusion(f32[1024,1024]{1,0:T(8,128)} %scatter_fusion, bf16[1024,1024]{1,0:T(8,128)(2,1)S(1)} %copy-done.5, f32[1024]{0:T(1024)S(1)} %add_rsqrt_fusion, f32[1024]{0:T(1024)S(1)} %convert_element_type.68), kind=kLoop, calls=%fused_computation.10 | loop fusion | flops 7337984 | bytes 6307840 | tf_op jit(solution)/shard_map/reduce_sum | solution.py:384
  104.0 24.3 %scatter_sum.1 = (f32[8,2048]{1,0:T(8,128)S(1)}, f32[8,128]{1,0:T(8,128)S(1)}) custom-call(bf16[4,4,4,2,8,2048]{5,4,3,2,1,0:T(8,128)(2,1)S(1)} %bitcast.66, f32[8,128]{1,0:T(8,128)S(1)} %bitcast.67), custom_call_target="tpu_custom_call" | custom-call | tf_op jit(solution)/shard_map/scatter_sum/pallas_call | solution.py:270
  129.0 2.8 %subtract_multiply_fusion = f32[1024,1024]{1,0:T(8,128)} fusion(f32[1024,1024]{1,0:T(8,128)S(1)} %copy-done.6, bf16[1024,1024]{1,0:T(8,128)(2,1)S(1)} %copy-done.5, f32[1024]{0:T(1024)S(1)} %broadcast_multiply_fusion, f32[1024]{0:T(1024)S(1)} %convert_element_type.68, f32[1024]{0:T(1024)S(1)} %add_rsqrt_fusion), kind=kLoop, calls=%fused_computation.11 | loop fusion | flops 6291456 | bytes 10498048 | tf_op jit(solution)/shard_map/mul | solution.py:386
  131.8 4.8 %scatter_custom_fusion.1 = f32[1024,1024]{1,0:T(8,128)} fusion(f32[1024,1024]{1,0:T(8,128)} %subtract_multiply_fusion, s32[8]{0:T(128)S(1)} %fusion.56, f32[8,1024]{1,0:T(8,128)S(1)} %get-tuple-element.25, f32[8]{0:T(128)S(1)} %fusion.43, f32[8]{0:T(128)S(1)} %add_rsqrt_fusion.1, bf16[8,1024]{1,0:T(8,128)(2,1)S(1)} %gather_fusion.2, ...), kind=kCustom, calls=%fused_computation.59 | custom fusion | flops 57344 | bytes 4244992 | tf_op jit(solution)/shard_map/scatter-add | solution.py:387
  136.6 3.8 %convert_element_type.87 = bf16[1024,1024]{1,0:T(8,128)(2,1)} convert(f32[1024,1024]{1,0:T(8,128)} %scatter_custom_fusion.1) | non-fusion elementwise | flops 1048576 | bytes 6291456 | tf_op jit(solution)/shard_map/convert_element_type | solution.py:387
  (37 shorter events, 4.6 us)
Async XLA Ops:
  6.5 8.9 %copy-start.4 = (bf16[1024,1024]{1,0:T(8,128)(2,1)S(1)}, bf16[1024,1024]{1,0:T(8,128)(2,1)}, u32[]{:S(2)}) copy-start(bf16[1024,1024]{1,0:T(8,128)(2,1)} %param.11) | copy-start | bytes 6291460
  15.4 5.2 %copy-start.1 = (bf16[8,1024]{1,0:T(8,128)(2,1)S(1)}, bf16[8,1024]{1,0:T(8,128)(2,1)}, u32[]{:S(2)}) copy-start(bf16[8,1024]{1,0:T(8,128)(2,1)} %key_ref.1) | copy-start | bytes 49156
  15.4 5.2 %copy-start.2 = (bf16[8,1024]{1,0:T(8,128)(2,1)S(1)}, bf16[8,1024]{1,0:T(8,128)(2,1)}, u32[]{:S(2)}) copy-start(bf16[8,1024]{1,0:T(8,128)(2,1)} %value_ref.1) | copy-start | bytes 49156
  52.3 1.9 %copy-start.3 = (bf16[4,4,4,2,8,2048]{5,4,3,2,1,0:T(8,128)(2,1)}, bf16[4,4,4,2,8,2048]{5,4,3,2,1,0:T(8,128)(2,1)S(1)}, u32[]{:S(2)}) copy-start(bf16[4,4,4,2,8,2048]{5,4,3,2,1,0:T(8,128)(2,1)S(1)} %get-tuple-element.9) | copy-start | bytes 12582916
  67.5 2.2 %copy-start.7 = (bf16[2048,1024]{1,0:T(8,128)(2,1)S(1)}, bf16[2048,1024]{1,0:T(8,128)(2,1)}, u32[]{:S(2)}) copy-start(bf16[2048,1024]{1,0:T(8,128)(2,1)} %param.19) | copy-start | bytes 12582916
  70.5 2.1 %copy-start.9 = (bf16[128,8,8,128]{3,2,1,0:T(8,128)(2,1)S(1)}, bf16[128,8,8,128]{3,2,1,0:T(8,128)(2,1)}, u32[]{:S(2)}) copy-start(bf16[128,8,8,128]{3,2,1,0:T(8,128)(2,1)} %copy.35) | copy-start | bytes 6291460
  78.0 1.4 copy-start.10
  79.4 8.5 %copy-start.8 = (bf16[1024,1024]{1,0:T(8,128)(2,1)S(1)}, bf16[1024,1024]{1,0:T(8,128)(2,1)}, u32[]{:S(2)}) copy-start(bf16[1024,1024]{1,0:T(8,128)(2,1)} %multiply_convert_fusion) | copy-start | bytes 6291460
  87.9 12.6 %copy-start.5 = (bf16[1024,1024]{1,0:T(8,128)(2,1)S(1)}, bf16[1024,1024]{1,0:T(8,128)(2,1)}, u32[]{:S(2)}) copy-start(bf16[1024,1024]{1,0:T(8,128)(2,1)} %param.11) | copy-start | bytes 6291460
  100.5 3.5 %copy-start = (bf16[1024,2048]{1,0:T(8,128)(2,1)S(1)}, bf16[1024,2048]{1,0:T(8,128)(2,1)}, u32[]{:S(2)}) copy-start(bf16[1024,2048]{1,0:T(8,128)(2,1)} %convolution_convert_fusion) | copy-start | bytes 12582916
  100.5 28.4 %copy-start.6 = (f32[1024,1024]{1,0:T(8,128)S(1)}, f32[1024,1024]{1,0:T(8,128)}, u32[]{:S(2)}) copy-start(f32[1024,1024]{1,0:T(8,128)} %scatter_fusion) | copy-start | bytes 12582916

commit v2 on v0

v2 whole, which is shorter than its diff:
```python
import functools
import jax
import jax.numpy as jnp
from jax import lax
from jax.experimental import pallas as pl
from jax.experimental.pallas import tpu as pltpu
from jax.sharding import PartitionSpec as P

QUERY_HEADS = 16
KEY_HEADS = 8
HEAD_WIDTH = 128
WIDTH = KEY_HEADS * HEAD_WIDTH
SLOTS = 8
TILE = 256
RING = 4
STRIDES = (32, 8, 2)
ORDERS = ((0, 1, 2), (1, 2, 0), (2, 0, 1))
MESH = pl.DeviceIdType.MESH
BF16, F32 = jnp.bfloat16, jnp.float32
GATHER_CUTS = (
    ((0, 384), (384, 384), (768, 256)),
    ((0, 256), (256, 384), (640, 384)),
    ((0, 384), (384, 256), (640, 384)),
)
SCATTER_CUTS = ((0, 768), (768, 640), (1408, 640))


def f32(value):
    return value.astype(F32)


def dot(a, b, ca=1, cb=0):
    return lax.dot_general(a, b, (((ca,), (cb,)), ((), ())), preferred_element_type=F32)


class Net:
    def __init__(self, sems):
        self.sems, self.used = sems, 0
        me = lax.axis_index("dp")
        self.me = me
        self.coords = ((me // 32) % RING, (me // 8) % RING, (me // 2) % RING)
        self.core = me % 2
        self.sibling = me + 1 - 2 * self.core

    def at(self, dim, delta):
        return (self.coords[dim] + delta + RING) % RING

    def peer(self, dim, delta):
        return self.me + (self.at(dim, delta) - self.coords[dim]) * STRIDES[dim]

    def greet(self):
        barrier = pltpu.get_barrier_semaphore()
        pl.semaphore_signal(barrier, inc=1, device_id=(self.sibling,), device_id_type=MESH)
        for dim in range(3):
            for delta in range(1, RING):
                pl.semaphore_signal(
                    barrier, inc=1, device_id=(self.peer(dim, delta),), device_id_type=MESH
                )
        pl.semaphore_wait(barrier, 10)

    def send(self, src, dst, other):
        copy = pltpu.make_async_remote_copy(
            src_ref=src,
            dst_ref=dst,
            send_sem=self.sems.at[0, self.used],
            recv_sem=self.sems.at[1, self.used],
            device_id=(other,),
            device_id_type=MESH,
        )
        self.used += 1
        copy.start()
        return copy

    def local(self, src, dst):
        copy = pltpu.make_async_copy(src, dst, self.sems.at[0, self.used])
        self.used += 1
        copy.start()
        return copy


def finish(copies):
    for copy in copies:
        copy.wait()
    copies.clear()


class Gather:
    def __init__(self, net, source, target, low, size, order):
        self.net, self.order = net, order
        self.source = source.at[:, pl.ds(low, size)]
        self.target = target.at[:, :, :, :, :, pl.ds(low, size)]
        self.flying, self.paired = [], []

    def slab(self, done, dim=None, delta=0, half=None):
        net = self.net
        index = [net.coords[0], net.coords[1], net.coords[2], net.core]
        if dim is not None:
            index[dim] = net.at(dim, delta)
        for at in done:
            index[at] = slice(None)
        if half is not None:
            index[done[0]] = pl.ds(half * 2, 2)
        return self.target.at[tuple(index)]

    def open(self):
        net, mine = self.net, self.slab(())
        self.own = net.local(self.source, mine)
        for delta in (2, 1, 3):
            self.flying.append(net.send(self.source, mine, net.peer(self.order[0], delta)))

    def pair(self, step, delta):
        piece = self.slab(self.order[:step], self.order[step], delta)
        self.paired.append(self.net.send(piece, piece, self.net.sibling))

    def ring(self, step):
        if step == 1:
            self.own.wait()
        finish(self.flying)
        dim, piece = self.order[step], self.slab(self.order[:step])
        for delta in (1, 3):
            self.flying.append(self.net.send(piece, piece, self.net.peer(dim, delta)))
        if step == 2:
            self.pair(2, 0)

    def relay(self, step):
        finish(self.flying)
        dim, done = self.order[step], self.order[:step]
        for half, delta in ((0, 1), (1, 3)):
            piece = self.slab(done, dim, RING - delta, half)
            self.flying.append(self.net.send(piece, piece, self.net.peer(dim, delta)))
        if step == 2:
            self.pair(2, 1)
            self.pair(2, 3)

    def close(self):
        finish(self.flying)
        self.pair(2, 2)


def step_kernel(
    lengths,
    owner,
    hidden_hbm,
    grad_ref,
    gain_ref,
    query_hbm,
    key_ref,
    value_ref,
    out_hbm,
    grad_in,
    weight_grad,
    gain_grad,
    *scratch,
):
    (hid, wq, wo, kv, every, grad_b, nb, nbt, inv_s, joint, both, result) = scratch[:12]
    (score, prob, gscore, q_all, a_all, flat, flat_b, select_rows, pool_rows) = scratch[12:21]
    (share, gain_acc, gain_pair, gain_sum, gain_in, sems) = scratch[21:27]
    pair_in, first, relay_in, first_in, second, second_in, third, third_in = (
        scratch[27 + 3 * i : 30 + 3 * i] for i in range(8)
    )
    net = Net(sems)
    scale_q = 1.0 / HEAD_WIDTH**0.5
    tokens = nb.shape[0]
    tiles = tokens // TILE
    blocks = TILE // SLOTS

    hid_copy = net.local(hidden_hbm, hid)
    wq_copy = net.local(query_hbm, wq)
    grad_b[...] = grad_ref[...].astype(BF16)
    net.greet()
    key_parts, value_parts, grad_parts = (
        [
            Gather(net, source, target, low, size, ORDERS[part])
            for part, (low, size) in enumerate(cuts)
        ]
        for source, target, cuts in (
            (key_ref, kv.at[:, :, :, :, :, pl.ds(0, WIDTH)], GATHER_CUTS[0]),
            (value_ref, kv.at[:, :, :, :, :, pl.ds(WIDTH, WIDTH)], GATHER_CUTS[1]),
            (grad_b, every, GATHER_CUTS[2]),
        )
    )
    for part in key_parts + value_parts + grad_parts:
        part.open()
    wo_copy = net.local(out_hbm, wo)
    gain = f32(gain_ref[...])

    def norm_tile(i):
        rows = pl.ds(pl.multiple_of(i * TILE, TILE), TILE)
        x = f32(hid[pl.ds(i * blocks, blocks)]).reshape(TILE, WIDTH)
        inv = lax.rsqrt(jnp.mean(x * x, axis=-1, keepdims=True) + 1e-06)
        inv_s[rows, :] = inv
        y = (x * inv) * gain
        nb[rows, :] = y.astype(BF16)
        nbt[:, rows] = y.T.astype(BF16)

    hid_copy.wait()

    @pl.loop(0, tiles // 2)
    def _(i):
        norm_tile(i)

    for part in key_parts:
        part.ring(1)
    for part in value_parts:
        part.ring(1)

    @pl.loop(tiles // 2, tiles)
    def _(i):
        norm_tile(i)

    for part in key_parts:
        part.relay(1)
    for part in value_parts:
        part.relay(1)

    row8 = lax.broadcasted_iota(jnp.int32, (SLOTS, WIDTH), 0)
    lane = lax.broadcasted_iota(jnp.int32, (SLOTS, WIDTH), 1)
    starts = jnp.zeros((SLOTS, WIDTH), jnp.int32)
    ends = jnp.zeros((SLOTS, WIDTH), jnp.int32)
    lane_last = jnp.full((SLOTS, HEAD_WIDTH), -1, jnp.int32)
    short_lane = lax.broadcasted_iota(jnp.int32, (SLOTS, HEAD_WIDTH), 1)
    hidden_last = jnp.zeros((SLOTS, WIDTH), F32)
    at = jnp.int32(0)
    for s in range(SLOTS):
        starts = jnp.where(row8 == s, at, starts)
        at = at + lengths[0, s]
        ends = jnp.where(row8 == s, at, ends)
        last = jnp.maximum(at - 1, 0)
        chosen = (short_lane % SLOTS == s) & (short_lane < 3 * SLOTS)
        lane_last = jnp.where(chosen, last, lane_last)
        block = f32(hid[last // SLOTS])
        picked = jnp.sum(jnp.where(row8 == last % SLOTS, block, 0.0), axis=0, keepdims=True)
        hidden_last = jnp.where(row8 == s, picked, hidden_last)
    member = (lane >= starts) & (lane < ends)
    inv_last = lax.rsqrt(jnp.mean(hidden_last * hidden_last, axis=-1, keepdims=True) + 1e-06)
    normed_last = hidden_last * inv_last
    last_b = (normed_last * gain).astype(BF16)

    for part in key_parts:
        part.ring(2)
    wq_copy.wait()

    def spread(value, at, target):
        for part in range(value.shape[1] // HEAD_WIDTH):
            target[pl.ds(SLOTS * (at + part), SLOTS), :] = f32(
                value[:, part * HEAD_WIDTH : (part + 1) * HEAD_WIDTH].astype(BF16)
            )

    for n in range(4):
        spread(dot(last_b, wq[:, pl.ds(512 * n, 512)]), 4 * n, q_all)
    for part in value_parts:
        part.ring(2)
    for part in key_parts:
        part.relay(2)
    for part in grad_parts:
        part.ring(1)
    for part in value_parts:
        part.relay(2)
    for part in key_parts:
        part.close()
    for part in grad_parts:
        part.relay(1)
    for part in key_parts:
        finish(part.paired)

    def project(i, low):
        rows = pl.ds(pl.multiple_of(i * TILE, TILE), TILE)
        weight = kv[:, :, :, :, :, pl.ds(low, WIDTH)].reshape(WIDTH, WIDTH)
        joint[rows, pl.ds(low, WIDTH)] = dot(nb[rows, :], weight).astype(BF16)

    @pl.loop(0, tiles // 2)
    def _(i):
        project(i, 0)

    for part in value_parts:
        part.close()
    for part in grad_parts:
        part.ring(2)

    @pl.loop(tiles // 2, tiles)
    def _(i):
        project(i, 0)

    for part in value_parts:
        finish(part.paired)
    for part in grad_parts:
        part.relay(2)

    @pl.loop(0, tiles)
    def _(i):
        project(i, WIDTH)

    for part in grad_parts:
        part.close()

    def head(g, base=0):
        return pl.ds(base + g * HEAD_WIDTH, HEAD_WIDTH)

    def pair_rows(g):
        return pl.ds(2 * SLOTS * g, 2 * SLOTS)

    for g in range(KEY_HEADS):
        score[pair_rows(g), :] = dot(q_all[pair_rows(g), :].astype(BF16), joint[:, head(g)], 1, 1)
    scores = score[...].reshape(QUERY_HEADS, SLOTS, tokens) * scale_q
    scores = jnp.where(member[None], scores, -1e30)
    expo = jnp.exp(scores - jnp.max(scores, axis=-1, keepdims=True))
    probs = expo / jnp.sum(expo, axis=-1, keepdims=True)
    prob[...] = probs.reshape(QUERY_HEADS * SLOTS, tokens)

    def flatten(g, value):
        for q in range(2):
            flat[:, head(2 * g + q)] = value[q * SLOTS : (q + 1) * SLOTS, :]

    for g in range(KEY_HEADS):
        flatten(g, dot(prob[pair_rows(g), :].astype(BF16), joint[:, head(g, WIDTH)]))
    wo_copy.wait()
    pooled = hidden_last + dot(flat[...].astype(BF16), wo[...])
    for part in grad_parts:
        finish(part.paired)
    cached = jnp.zeros((SLOTS, WIDTH), F32)
    for s in range(SLOTS):
        o = owner[s]
        block = f32(every[o // 256, (o // 64) % RING, (o // 16) % RING, (o // 8) % 2])
        picked = jnp.sum(jnp.where(row8 == o % SLOTS, block, 0.0), axis=0, keepdims=True)
        cached = jnp.where(row8 == s, picked, cached)
    inv_len = lax.rsqrt(jnp.sum(pooled * pooled, axis=-1, keepdims=True) + 1e-06)
    embed = pooled * inv_len
    grad_pool = inv_len * (cached - embed * jnp.sum(embed * cached, axis=-1, keepdims=True))
    grad_pool_b = grad_pool.astype(BF16)
    for n in range(4):
        spread(dot(grad_pool_b, wo[pl.ds(512 * n, 512), :], 1, 1), 4 * n, a_all)

    def three(value):
        hi = f32(value.astype(BF16))
        mid = f32((value - hi).astype(BF16))
        rest = jnp.zeros((HEAD_WIDTH - 3 * SLOTS, WIDTH), F32)
        return jnp.concatenate([hi, mid, (value - hi) - mid, rest], axis=0).astype(BF16)

    pool_rows[...] = three(grad_pool)

    for g in range(KEY_HEADS):
        score[pair_rows(g), :] = dot(
            a_all[pair_rows(g), :].astype(BF16), joint[:, head(g, WIDTH)], 1, 1
        )
        both[:, head(g, WIDTH)] = dot(
            prob[pair_rows(g), :].astype(BF16), a_all[pair_rows(g), :].astype(BF16), 0, 0
        ).astype(BF16)
    grad_prob = score[...]
    probs = prob[...]
    inner = jnp.sum(probs * grad_prob, axis=-1, keepdims=True)
    gscore[...] = (probs * (grad_prob - inner) * scale_q).astype(BF16)
    for g in range(KEY_HEADS):
        both[:, head(g)] = dot(
            gscore[pair_rows(g), :], q_all[pair_rows(g), :].astype(BF16), 0, 0
        ).astype(BF16)

    def share_part(part):
        low, size = SCATTER_CUTS[part]

        @pl.loop(0, RING)
        def _(x):
            rows = pl.ds(pl.multiple_of(x * TILE, TILE), TILE)
            value = dot(nbt[rows, :], both[:, pl.ds(low, size)])
            share[x, :, :, :, :, pl.ds(low, size)] = value.reshape(
                RING, RING, 2, SLOTS, size
            ).astype(BF16)
            weight = f32(kv[x, :, :, :, :, pl.ds(low, size)]).reshape(TILE, size)
            product = value * weight
            total = product[:, :HEAD_WIDTH]
            for n in range(1, size // HEAD_WIDTH):
                total = total + product[:, n * HEAD_WIDTH : (n + 1) * HEAD_WIDTH]
            if part == 0:
                gain_acc[rows, :] = total
            else:
                gain_acc[rows, :] += total

        return net.send(
            share.at[:, :, :, 1 - net.core, :, pl.ds(low, size)], pair_in[part], net.sibling
        )

    flights = [[], [], []]
    early = [[], [], []]

    def halves(part):
        pairs[part].wait()
        low, size = SCATTER_CUTS[part]
        order = ORDERS[part]

        @pl.loop(0, RING * RING)
        def _(at):
            ahead = [at // RING, at % RING, 0]
            for z in range(RING):
                ahead[2] = z
                value = f32(share[ahead[0], ahead[1], z, net.core, :, pl.ds(low, size)])
                value = value + f32(pair_in[part][ahead[0], ahead[1], z])
                first[part][ahead[order[0]], ahead[order[1]], ahead[order[2]]] = value.astype(BF16)

        dim = order[0]
        for half, delta in ((0, 1), (1, 3)):
            flights[part].append(
                net.send(
                    first[part].at[net.at(dim, 2), pl.ds(2 * half, 2)],
                    relay_in[part].at[half],
                    net.peer(dim, delta),
                )
            )
            early[part].append(
                net.send(
                    first[part].at[net.at(dim, delta), pl.ds(2 - 2 * half, 2)],
                    first_in[part].at[half, pl.ds(2 - 2 * half, 2)],
                    net.peer(dim, delta),
                )
            )

    def passed(part):
        finish(flights[part])
        dim = ORDERS[part][0]
        for half, delta in ((0, 1), (1, 3)):
            there = net.at(dim, delta)
            for a in range(2):
                row = 2 * half + a
                value = f32(first[part][there, row]) + f32(relay_in[part][half, a])
                first[part][there, row] = value.astype(BF16)
            flights[part].append(
                net.send(
                    first[part].at[there, pl.ds(2 * half, 2)],
                    first_in[part].at[half, pl.ds(2 * half, 2)],
                    net.peer(dim, delta),
                )
            )

    def push(part, step, source, target):
        dim = ORDERS[part][step]
        for delta in (2, 1, 3):
            flights[part].append(
                net.send(source.at[net.at(dim, delta)], target.at[delta - 1], net.peer(dim, delta))
            )

    def summed(part):
        finish(flights[part])
        finish(early[part])
        mine = net.coords[ORDERS[part][0]]
        for a in range(RING):
            value = f32(first[part][mine, a])
            value = value + (f32(first_in[part][0, a]) + f32(first_in[part][1, a]))
            second[part][a] = value.astype(BF16)
        push(part, 1, second[part], second_in[part])

    def summed_again(part):
        finish(flights[part])
        mine = net.coords[ORDERS[part][1]]
        value = f32(second[part][mine]) + f32(second_in[part][0])
        value = value + (f32(second_in[part][1]) + f32(second_in[part][2]))
        third[part][...] = value.astype(BF16)
        push(part, 2, third[part], third_in[part])

    def summed_last(part):
        low, size = SCATTER_CUTS[part]
        finish(flights[part])
        mine = net.coords[ORDERS[part][2]]
        value = f32(third[part][mine]) + f32(third_in[part][0])
        value = value + (f32(third_in[part][1]) + f32(third_in[part][2]))
        weight_grad[:, pl.ds(low, size)] = value

    def gain_round(dim, value):
        gain_sum[dim + 1] = value
        gain_in[dim, net.coords[dim]] = value
        return [
            net.send(
                gain_sum.at[dim + 1], gain_in.at[dim, net.coords[dim]], net.peer(dim, delta)
            )
            for delta in range(1, RING)
        ]

    def gain_total(dim, copies):
        finish(copies)
        return (gain_in[dim, 0] + gain_in[dim, 1]) + (gain_in[dim, 2] + gain_in[dim, 3])

    out_copies = []

    def input_grad(i):
        rows = pl.ds(i * TILE, TILE)
        weight = kv[...].reshape(WIDTH, 2 * WIDTH)
        tall = lax.broadcasted_iota(jnp.int32, (TILE, HEAD_WIDTH), 0) + i * TILE
        hot = jnp.where(tall == lane_last[:1], 1.0, 0.0).astype(BF16)
        grad_normed = dot(both[rows, :], weight, 1, 1) + dot(hot, select_rows[...])
        inv = inv_s[rows, :]
        normed = f32(hid[pl.ds(i * blocks, blocks)]).reshape(TILE, WIDTH) * inv
        scaled = grad_normed * gain
        mean = jnp.mean(scaled * normed, axis=-1, keepdims=True)
        value = inv * (scaled - normed * mean) + dot(hot, pool_rows[...])
        result[rows, :] = value.astype(BF16)
        out_copies.append(net.local(result.at[rows], grad_in.at[rows]))

    pairs = [share_part(0), share_part(1)]
    halves(0)
    pairs.append(share_part(2))
    halves(1)
    for g in range(KEY_HEADS):
        flatten(g, dot(gscore[pair_rows(g), :], joint[:, head(g)]))
    query_back = dot(flat[...].astype(BF16), wq[...], 1, 1)
    select_rows[...] = three(query_back)
    gain_part = jnp.sum(gain_acc[...].T, axis=0, keepdims=True) / gain
    gain_part = gain_part + jnp.sum(query_back * normed_last, axis=0, keepdims=True)
    gain_sum[0] = gain_part
    gain_copies = [net.send(gain_sum.at[0], gain_pair, net.sibling)]
    halves(2)
    passed(0)
    input_grad(0)
    finish(gain_copies)
    gain_copies = gain_round(0, gain_sum[0] + gain_pair[...])
    passed(1)
    passed(2)
    summed(0)
    input_grad(1)
    gain_copies = gain_round(1, gain_total(0, gain_copies))
    summed(1)
    summed(2)
    summed_again(0)
    input_grad(2)
    gain_copies = gain_round(2, gain_total(1, gain_copies))
    summed_again(1)
    summed_again(2)
    input_grad(3)
    gain_grad[...] = gain_total(2, gain_copies)
    for part in range(3):
        summed_last(part)
    finish(out_copies)


def per_device(
    hidden_in, lengths, owner, pooled_grad, norm_gain, w_query, w_key, value_weight, w_out
):
    tokens, width = hidden_in.shape
    heads = QUERY_HEADS * SLOTS
    grid = (RING, RING, RING, 2, SLOTS)

    def vmem(*shape, kind=BF16):
        return pltpu.VMEM(shape, kind)

    def parts(*lead):
        return [vmem(*lead, SLOTS, size) for _, size in SCATTER_CUTS]

    spec = pl.BlockSpec(memory_space=pltpu.VMEM)
    smem = pl.BlockSpec(memory_space=pltpu.SMEM)
    hbm = pl.BlockSpec(memory_space=pl.ANY)
    grad_in, weight_grad, gain_grad = pl.pallas_call(
        step_kernel,
        out_shape=(
            jax.ShapeDtypeStruct((tokens, width), BF16),
            jax.ShapeDtypeStruct((SLOTS, 2 * WIDTH), F32),
            jax.ShapeDtypeStruct((1, width), F32),
        ),
        in_specs=[smem, smem, hbm, spec, spec, hbm, spec, spec, hbm],
        out_specs=(hbm, spec, spec),
        scratch_shapes=[
            vmem(tokens // SLOTS, SLOTS, width),
            vmem(width, 2 * WIDTH),
            vmem(2 * WIDTH, width),
            vmem(*grid, 2 * WIDTH),
            vmem(*grid, width),
            vmem(SLOTS, width),
            vmem(tokens, width),
            vmem(width, tokens),
            vmem(tokens, 1, kind=F32),
            vmem(tokens, 2 * WIDTH),
            vmem(tokens, 2 * WIDTH),
            vmem(tokens, width),
            vmem(heads, tokens, kind=F32),
            vmem(heads, tokens, kind=F32),
            vmem(heads, tokens),
            vmem(heads, HEAD_WIDTH, kind=F32),
            vmem(heads, HEAD_WIDTH, kind=F32),
            vmem(SLOTS, 2 * WIDTH, kind=F32),
            vmem(SLOTS, 2 * WIDTH),
            vmem(HEAD_WIDTH, width),
            vmem(HEAD_WIDTH, width),
            vmem(*grid, 2 * WIDTH),
            vmem(width, HEAD_WIDTH, kind=F32),
            vmem(1, width, kind=F32),
            vmem(4, 1, width, kind=F32),
            vmem(3, RING, 1, width, kind=F32),
            pltpu.SemaphoreType.DMA((2, 256)),
        ]
        + parts(RING, RING, RING)
        + parts(RING, RING, RING)
        + parts(2, 2, RING)
        + parts(2, RING, RING)
        + parts(RING, RING)
        + parts(RING - 1, RING)
        + parts(RING)
        + parts(RING - 1),
        compiler_params=pltpu.CompilerParams(
            collective_id=0, has_side_effects=True, vmem_limit_bytes=60 * 2**20
        ),
        name="step",
    )(
        lengths,
        owner,
        hidden_in.reshape(tokens // SLOTS, SLOTS, width),
        pooled_grad,
        norm_gain.reshape(1, width),
        w_query,
        w_key,
        value_weight,
        w_out,
    )
    return grad_in, weight_grad[:, :WIDTH], weight_grad[:, WIDTH:], gain_grad.reshape(-1)


def solution(mesh):
    return jax.shard_map(
        per_device,
        mesh=mesh,
        in_specs=(
            P("dp", None),
            P("dp", None),
            P("dp"),
            P("dp", None),
            P(),
            P(),
            P("dp", None),
            P("dp", None),
            P(),
        ),
        out_specs=(P("dp", None), P("dp", None), P("dp", None), P()),
        check_vma=False,
    )
```

time: 841 us -> 83.1 us (0.10)
  waiting for transfers between devices: 665 us -> 0 us
  Pallas kernels: 0 us -> 75.8 us
  blocking collectives: 64 us -> 0 us
  matrix products: 47.4 us -> 0 us
  other arithmetic: 34.3 us -> 0 us
  between operations: 13.9 us -> 0.64 us
  local copies, waits for them, and re-layouts: 15.1 us -> 6.36 us
    reduce_scatter x1 -> x0, waiting for transfers between devices: 550 us -> none  [per_device(): lax.psum_scatter(lax.dot_general(normed_b, grad_both, (((0,), (0,)), ((),...]
    all_gather x2 -> x0, waiting for transfers between devices: 115 us -> none  [the longest x1 61.3 us: per_device(): kv_full = lax.all_gather(kv_rows, 'dp', axis=0, tiled=True)]
    pallas_call x0 -> x1, Pallas kernels: none -> 75.8 us  [per_device(): pl.pallas_call(step_kernel, out_shape=(jax.ShapeDtypeStruct((tokens, widt...]
    psum x1 -> x0, blocking collectives: 64 us -> none  [per_device(): gain_total = lax.psum(jnp.sum(grad_normed * normed, axis=0), 'dp')]
    dot_general x12 -> x0, matrix products: 45 us -> none  [the longest x1 10.6 us: per_device(): lax.dot_general(normed_b, grad_both, (((0,), (0,)), ((), ())), preferred_...]
    convert_element_type x6 -> x0, other arithmetic: 15.9 us -> none  [the longest x1 3.98 us: per_device(): inputs_f = hidden_in.astype(jnp.float32)]
    scatter-add x2 -> x0, other arithmetic: 9.64 us -> none  [the longest x1 4.87 us: per_device(): grad_in = grad_in.at[last_rows].add(grad_pool).astype(jnp.bfloat16)]
  transfers between devices with their start and end apart: 3 -> 0, of which waited for: 3 -> 0; matrix products, arithmetic and copies ran while one was open for 7% -> 0% of each run, Pallas kernels for 0% -> 0%
where the time goes in v2:
time: 83.1 us; the launch traced here: 82.8 us
  Pallas kernels  75.8 us (91%)
  local copies, waits for them, and re-layouts  6.36 us (8%)
    pallas_call x1, Pallas kernels, per_device(): pl.pallas_call(step_kernel, out_shape=(jax.ShapeDtypeStruct((tokens, widt...  75.8 us
    unnamed x4, local copies, waits for them, and re-layouts  3.68 us

profile of v2, /device:TPU:0, one launch (start us, length us, event | category | flops | bytes accessed | tf_op | source)
XLA Modules:
  0.0 82.8 jit_solution(11530600712910356202)
XLA Ops:
  0.6 1.3 %reshape.18.gain_ref = bf16[1,1024]{1,0:T(2,128)(2,1)} reshape(bf16[1024]{0:T(1024)(128)(2,1)} %param.13) | data formatting | bytes 4096 | tf_op jit(solution)/shard_map/reshape | solution.py:602
  1.9 75.8 %step.1 = (bf16[1024,1024]{1,0:T(8,128)(2,1)}, f32[8,2048]{1,0:T(8,128)}, f32[1,1024]{1,0:T(1,128)}) custom-call(s32[1,8]{1,0:T(1,128)} %lengths.1, s32[8]{0:T(128)} %owner.1, bf16[128,8,1024]{2,1,0:T(8,128)(2,1)} %bitcast.2, f32[8,1024]{1,0:T(8,128)} %grad_ref.1, bf16[1,1024]{1,0:T(2,128)(2,1)} %reshape.18.gain_ref, bf16[1024,2048]{1,0:T(8,128)(2,1)} %query_hbm.1, ...), custom_call_target="tpu_custom_call" | custom-call | tf_op jit(solution)/shard_map/step/pallas_call | solution.py:547
  77.7 1.4 %fusion = (f32[8,1024]{1,0:T(8,128)}, f32[8,1024]{1,0:T(8,128)}) fusion(f32[8,2048]{1,0:T(8,128)} %get-tuple-element.8), kind=kLoop, calls=%fused_computation | loop fusion | bytes 131072 | tf_op jit(solution)/shard_map/slice | solution.py:608
  79.1 0.0 copy-start
  79.1 3.1 %copy.15 = bf16[1024,1024]{1,0:T(8,128)(2,1)} copy(bf16[1024,1024]{1,0:T(8,128)(2,1)} %get-tuple-element.16) | data formatting | bytes 4194304
  82.2 0.0 copy-done
  82.2 0.6 copy.16
Async XLA Ops:
  79.1 3.1 %copy-start = (f32[1,1024]{1,0:T(1,128)S(1)}, f32[1,1024]{1,0:T(1,128)}, u32[]{:S(2)}) copy-start(f32[1,1024]{1,0:T(1,128)} %get-tuple-element.9) | copy-start | bytes 12292

commit v3 on v2

--- a/solution.py
+++ b/solution.py
@@ -117,39 +117,35 @@
             self.own.wait()
         finish(self.flying)
         dim, piece = self.order[step], self.slab(self.order[:step])
-        for delta in (1, 3):
+        for delta in (2, 1, 3):
             self.flying.append(self.net.send(piece, piece, self.net.peer(dim, delta)))
         if step == 2:
             self.pair(2, 0)
 
     def relay(self, step):
-        finish(self.flying)
-        dim, done = self.order[step], self.order[:step]
-        for half, delta in ((0, 1), (1, 3)):
-            piece = self.slab(done, dim, RING - delta, half)
-            self.flying.append(self.net.send(piece, piece, self.net.peer(dim, delta)))
         if step == 2:
+            self.flying[1].wait()
+            self.pair(2, 3)
+            self.flying[2].wait()
             self.pair(2, 1)
-            self.pair(2, 3)
 
     def close(self):
-        finish(self.flying)
+        self.flying[0].wait()
         self.pair(2, 2)
 
 
 def step_kernel(
-    lengths,
-    owner,
+    lengths_hbm,
+    owner_hbm,
     hidden_hbm,
-    grad_ref,
-    gain_ref,
+    grad_hbm,
+    gain_hbm,
     query_hbm,
-    key_ref,
-    value_ref,
+    key_hbm,
+    value_hbm,
     out_hbm,
     grad_in,
-    weight_grad,
-    gain_grad,
+    packed,
     *scratch,
 ):
     (hid, wq, wo, kv, every, grad_b, nb, nbt, inv_s, joint, both, result) = scratch[:12]
@@ -158,15 +154,36 @@
     pair_in, first, relay_in, first_in, second, second_in, third, third_in = (
         scratch[27 + 3 * i : 30 + 3 * i] for i in range(8)
     )
+    lengths, owner, grad_f, gain_ref, key_ref, value_ref, hid_sems = scratch[51:]
     net = Net(sems)
     scale_q = 1.0 / HEAD_WIDTH**0.5
     tokens = nb.shape[0]
     tiles = tokens // TILE
     blocks = TILE // SLOTS
 
-    hid_copy = net.local(hidden_hbm, hid)
-    wq_copy = net.local(query_hbm, wq)
-    grad_b[...] = grad_ref[...].astype(BF16)
+    key_copy = net.local(key_hbm, key_ref)
+    value_copy = net.local(value_hbm, value_ref)
+    grad_copy = net.local(grad_hbm, grad_f)
+    small = [
+        net.local(gain_hbm, gain_ref),
+        net.local(lengths_hbm, lengths),
+        net.local(owner_hbm, owner),
+    ]
+
+    def hid_copy(i):
+        part = pl.ds(i * blocks, blocks)
+        return pltpu.make_async_copy(hidden_hbm.at[part], hid.at[part], hid_sems.at[i])
+
+    for i in range(tiles):
+        hid_copy(i).start()
+
+    def load(src, dst):
+        rows = dst.shape[0] // 4
+        return [
+            net.local(src.at[pl.ds(n * rows, rows)], dst.at[pl.ds(n * rows, rows)])
+            for n in range(4)
+        ]
+
     net.greet()
     key_parts, value_parts, grad_parts = (
         [
@@ -179,12 +196,21 @@
             (grad_b, every, GATHER_CUTS[2]),
         )
     )
-    for part in key_parts + value_parts + grad_parts:
+    key_copy.wait()
+    for part in key_parts:
         part.open()
-    wo_copy = net.local(out_hbm, wo)
-    gain = f32(gain_ref[...])
+    value_copy.wait()
+    for part in value_parts:
+        part.open()
+    grad_copy.wait()
+    grad_b[...] = grad_f[...].astype(BF16)
+    for part in grad_parts:
+        part.open()
+    finish(small)
+    gain = f32(gain_ref[...]).reshape(1, WIDTH)
 
     def norm_tile(i):
+        hid_copy(i).wait()
         rows = pl.ds(pl.multiple_of(i * TILE, TILE), TILE)
         x = f32(hid[pl.ds(i * blocks, blocks)]).reshape(TILE, WIDTH)
         inv = lax.rsqrt(jnp.mean(x * x, axis=-1, keepdims=True) + 1e-06)
@@ -193,8 +219,6 @@
         nb[rows, :] = y.astype(BF16)
         nbt[:, rows] = y.T.astype(BF16)
 
-    hid_copy.wait()
-
     @pl.loop(0, tiles // 2)
     def _(i):
         norm_tile(i)
@@ -208,10 +232,13 @@
     def _(i):
         norm_tile(i)
 
+    wq_copy = load(query_hbm, wq)
     for part in key_parts:
-        part.relay(1)
+        part.ring(2)
     for part in value_parts:
-        part.relay(1)
+        part.ring(2)
+    for part in grad_parts:
+        part.ring(1)
 
     row8 = lax.broadcasted_iota(jnp.int32, (SLOTS, WIDTH), 0)
     lane = lax.broadcasted_iota(jnp.int32, (SLOTS, WIDTH), 1)
@@ -236,9 +263,7 @@
     normed_last = hidden_last * inv_last
     last_b = (normed_last * gain).astype(BF16)
 
-    for part in key_parts:
-        part.ring(2)
-    wq_copy.wait()
+    finish(wq_copy)
 
     def spread(value, at, target):
         for part in range(value.shape[1] // HEAD_WIDTH):
@@ -248,18 +273,15 @@
 
     for n in range(4):
         spread(dot(last_b, wq[:, pl.ds(512 * n, 512)]), 4 * n, q_all)
-    for part in value_parts:
-        part.ring(2)
     for part in key_parts:
         part.relay(2)
     for part in grad_parts:
-        part.ring(1)
+        part.ring(2)
+    for part in key_parts:
+        part.close()
     for part in value_parts:
         part.relay(2)
-    for part in key_parts:
-        part.close()
-    for part in grad_parts:
-        part.relay(1)
+    wo_copy = load(out_hbm, wo)
     for part in key_parts:
         finish(part.paired)
 
@@ -274,8 +296,6 @@
 
     for part in value_parts:
         part.close()
-    for part in grad_parts:
-        part.ring(2)
 
     @pl.loop(tiles // 2, tiles)
     def _(i):
@@ -313,7 +333,7 @@
 
     for g in range(KEY_HEADS):
         flatten(g, dot(prob[pair_rows(g), :].astype(BF16), joint[:, head(g, WIDTH)]))
-    wo_copy.wait()
+    finish(wo_copy)
     pooled = hidden_last + dot(flat[...].astype(BF16), wo[...])
     for part in grad_parts:
         finish(part.paired)
@@ -460,7 +480,7 @@
         mine = net.coords[ORDERS[part][2]]
         value = f32(third[part][mine]) + f32(third_in[part][0])
         value = value + (f32(third_in[part][1]) + f32(third_in[part][2]))
-        weight_grad[:, pl.ds(low, size)] = value
+        packed[:SLOTS, pl.ds(low, size)] = value
 
     def gain_round(dim, value):
         gain_sum[dim + 1] = value
@@ -522,7 +542,7 @@
     summed_again(1)
     summed_again(2)
     input_grad(3)
-    gain_grad[...] = gain_total(2, gain_copies)
+    packed[SLOTS : SLOTS + 1, :WIDTH] = gain_total(2, gain_copies)
     for part in range(3):
         summed_last(part)
     finish(out_copies)
@@ -542,17 +562,16 @@
         return [vmem(*lead, SLOTS, size) for _, size in SCATTER_CUTS]
 
     spec = pl.BlockSpec(memory_space=pltpu.VMEM)
-    smem = pl.BlockSpec(memory_space=pltpu.SMEM)
-    hbm = pl.BlockSpec(memory_space=pl.ANY)
-    grad_in, weight_grad, gain_grad = pl.pallas_call(
+    hbm = pl.BlockSpec(memory_space=pltpu.HBM)
+    whole = pl.BlockSpec(memory_space=pl.ANY)
+    grad_in, packed = pl.pallas_call(
         step_kernel,
         out_shape=(
             jax.ShapeDtypeStruct((tokens, width), BF16),
-            jax.ShapeDtypeStruct((SLOTS, 2 * WIDTH), F32),
-            jax.ShapeDtypeStruct((1, width), F32),
+            jax.ShapeDtypeStruct((2 * SLOTS, 2 * WIDTH), F32),
         ),
-        in_specs=[smem, smem, hbm, spec, spec, hbm, spec, spec, hbm],
-        out_specs=(hbm, spec, spec),
+        in_specs=[hbm] * 9,
+        out_specs=(whole, spec),
         scratch_shapes=[
             vmem(tokens // SLOTS, SLOTS, width),
             vmem(width, 2 * WIDTH),
@@ -589,23 +608,37 @@
         + parts(RING, RING)
         + parts(RING - 1, RING)
         + parts(RING)
-        + parts(RING - 1),
+        + parts(RING - 1)
+        + [
+            pltpu.SMEM((1, SLOTS), jnp.int32),
+            pltpu.SMEM((SLOTS,), jnp.int32),
+            vmem(SLOTS, width, kind=F32),
+            vmem(width),
+            vmem(SLOTS, WIDTH),
+            vmem(SLOTS, WIDTH),
+            pltpu.SemaphoreType.DMA((tokens // TILE,)),
+        ],
         compiler_params=pltpu.CompilerParams(
-            collective_id=0, has_side_effects=True, vmem_limit_bytes=60 * 2**20
+            collective_id=0, has_side_effects=True, vmem_limit_bytes=50 * 2**20
         ),
         name="step",
     )(
-        lengths,
-        owner,
-        hidden_in.reshape(tokens // SLOTS, SLOTS, width),
-        pooled_grad,
-        norm_gain.reshape(1, width),
-        w_query,
-        w_key,
-        value_weight,
-        w_out,
+        *(
+            pltpu.with_memory_space_constraint(value, pltpu.HBM)
+            for value in (
+                lengths,
+                owner,
+                hidden_in.reshape(tokens // SLOTS, SLOTS, width),
+                pooled_grad,
+                norm_gain,
+                w_query,
+                w_key,
+                value_weight,
+                w_out,
+            )
+        )
     )
-    return grad_in, weight_grad[:, :WIDTH], weight_grad[:, WIDTH:], gain_grad.reshape(-1)
+    return grad_in, packed[:SLOTS, :WIDTH], packed[:SLOTS, WIDTH:], packed[SLOTS, :WIDTH]
 
 
 def solution(mesh):

time: 83.1 us -> 73.2 us (0.88)
  Pallas kernels: 75.8 us -> 69.9 us
  local copies, waits for them, and re-layouts: 6.36 us -> 2.54 us
    pallas_call x1, Pallas kernels: 75.8 us -> 69.9 us  [per_device(): pl.pallas_call(step_kernel, out_shape=(jax.ShapeDtypeStruct((tokens, widt...]
    unnamed x4 -> x1, local copies, waits for them, and re-layouts: 3.68 us -> 1.32 us
    reshape x1 -> x0, local copies, waits for them, and re-layouts: 1.28 us -> none  [per_device(): norm_gain.reshape(1, width)]
where the time goes in v3:
time: 73.2 us; the launch traced here: 73.1 us
  Pallas kernels  69.9 us (95%)
  local copies, waits for them, and re-layouts  2.54 us (3%)
    pallas_call x1, Pallas kernels, per_device(): pl.pallas_call(step_kernel, out_shape=(jax.ShapeDtypeStruct((tokens, widt...  69.9 us

profile of v3, /device:TPU:0, one launch (start us, length us, event | category | flops | bytes accessed | tf_op | source)
XLA Modules:
  0.0 73.1 jit_solution(2571966630050624742)
XLA Ops:
  0.6 69.9 %step.1 = (bf16[1024,1024]{1,0:T(8,128)(2,1)S(1)}, f32[16,2048]{1,0:T(8,128)S(1)}) custom-call(s32[1,8]{1,0:T(1,128)} %lengths_hbm.1, s32[8]{0:T(128)} %owner_hbm.1, bf16[128,8,1024]{2,1,0:T(8,128)(2,1)} %bitcast.2, f32[8,1024]{1,0:T(8,128)} %grad_hbm.1, bf16[1024]{0:T(1024)(128)(2,1)} %gain_hbm.1, bf16[1024,2048]{1,0:T(8,128)(2,1)} %query_hbm.1, ...), custom_call_target="tpu_custom_call" | custom-call | tf_op jit(solution)/shard_map/step/pallas_call | solution.py:567
  70.5 0.6 fusion
  71.2 0.6 slice.11
  71.8 1.3 %copy.14 = bf16[1024,1024]{1,0:T(8,128)(2,1)} copy(bf16[1024,1024]{1,0:T(8,128)(2,1)S(1)} %get-tuple-element.14) | data formatting | bytes 4194304

commit v4 on v3

--- a/solution.py
+++ b/solution.py
@@ -22,7 +22,7 @@
     ((0, 256), (256, 384), (640, 384)),
     ((0, 384), (384, 256), (640, 384)),
 )
-SCATTER_CUTS = ((0, 768), (768, 640), (1408, 640))
+SCATTER_CUTS = ((0, 768), (768, 768), (1536, 512))
 
 
 def f32(value):

time: 73.2 us -> 71.5 us (0.977)
  Pallas kernels: 69.9 us -> 68.2 us
    pallas_call x1, Pallas kernels: 69.9 us -> 68.2 us  [per_device(): pl.pallas_call(step_kernel, out_shape=(jax.ShapeDtypeStruct((tokens, widt...]
where the time goes in v4:
time: 71.5 us; the launch traced here: 71.4 us
  Pallas kernels  68.2 us (95%)
  local copies, waits for them, and re-layouts  2.54 us (4%)
    pallas_call x1, Pallas kernels, per_device(): pl.pallas_call(step_kernel, out_shape=(jax.ShapeDtypeStruct((tokens, widt...  68.2 us

profile of v4, /device:TPU:0, one launch (start us, length us, event | category | flops | bytes accessed | tf_op | source)
XLA Modules:
  0.0 71.4 jit_solution(14026221278876750639)
XLA Ops:
  0.6 68.2 %step.1 = (bf16[1024,1024]{1,0:T(8,128)(2,1)S(1)}, f32[16,2048]{1,0:T(8,128)S(1)}) custom-call(s32[1,8]{1,0:T(1,128)} %lengths_hbm.1, s32[8]{0:T(128)} %owner_hbm.1, bf16[128,8,1024]{2,1,0:T(8,128)(2,1)} %bitcast.2, f32[8,1024]{1,0:T(8,128)} %grad_hbm.1, bf16[1024]{0:T(1024)(128)(2,1)} %gain_hbm.1, bf16[1024,2048]{1,0:T(8,128)(2,1)} %query_hbm.1, ...), custom_call_target="tpu_custom_call" | custom-call | tf_op jit(solution)/shard_map/step/pallas_call | solution.py:567
  68.9 0.6 fusion
  69.5 0.6 slice.11
  70.1 1.3 %copy.14 = bf16[1024,1024]{1,0:T(8,128)(2,1)} copy(bf16[1024,1024]{1,0:T(8,128)(2,1)S(1)} %get-tuple-element.14) | data formatting | bytes 4194304

commit v5 on v4

--- a/solution.py
+++ b/solution.py
@@ -17,11 +17,8 @@
 ORDERS = ((0, 1, 2), (1, 2, 0), (2, 0, 1))
 MESH = pl.DeviceIdType.MESH
 BF16, F32 = jnp.bfloat16, jnp.float32
-GATHER_CUTS = (
-    ((0, 384), (384, 384), (768, 256)),
-    ((0, 256), (256, 384), (640, 384)),
-    ((0, 384), (384, 256), (640, 384)),
-)
+WEIGHT_CUTS = ((0, 768), (768, 640), (1408, 640))
+GRAD_CUTS = ((0, 256), (256, 384), (640, 384))
 SCATTER_CUTS = ((0, 768), (768, 768), (1536, 512))
 
 
@@ -154,15 +151,17 @@
     pair_in, first, relay_in, first_in, second, second_in, third, third_in = (
         scratch[27 + 3 * i : 30 + 3 * i] for i in range(8)
     )
-    lengths, owner, grad_f, gain_ref, key_ref, value_ref, hid_sems = scratch[51:]
+    lengths, owner, grad_f, gain_ref, weight_ref, hid_sems = scratch[51:]
     net = Net(sems)
     scale_q = 1.0 / HEAD_WIDTH**0.5
     tokens = nb.shape[0]
     tiles = tokens // TILE
     blocks = TILE // SLOTS
 
-    key_copy = net.local(key_hbm, key_ref)
-    value_copy = net.local(value_hbm, value_ref)
+    weight_copies = [
+        net.local(key_hbm, weight_ref.at[:, pl.ds(0, WIDTH)]),
+        net.local(value_hbm, weight_ref.at[:, pl.ds(WIDTH, WIDTH)]),
+    ]
     grad_copy = net.local(grad_hbm, grad_f)
     small = [
         net.local(gain_hbm, gain_ref),
@@ -185,22 +184,18 @@
         ]
 
     net.greet()
-    key_parts, value_parts, grad_parts = (
+    weight_parts, grad_parts = (
         [
             Gather(net, source, target, low, size, ORDERS[part])
             for part, (low, size) in enumerate(cuts)
         ]
         for source, target, cuts in (
-            (key_ref, kv.at[:, :, :, :, :, pl.ds(0, WIDTH)], GATHER_CUTS[0]),
-            (value_ref, kv.at[:, :, :, :, :, pl.ds(WIDTH, WIDTH)], GATHER_CUTS[1]),
-            (grad_b, every, GATHER_CUTS[2]),
+            (weight_ref, kv, WEIGHT_CUTS),
+            (grad_b, every, GRAD_CUTS),
         )
     )
-    key_copy.wait()
-    for part in key_parts:
-        part.open()
-    value_copy.wait()
-    for part in value_parts:
+    finish(weight_copies)
+    for part in weight_parts:
         part.open()
     grad_copy.wait()
     grad_b[...] = grad_f[...].astype(BF16)
@@ -223,9 +218,7 @@
     def _(i):
         norm_tile(i)
 
-    for part in key_parts:
-        part.ring(1)
-    for part in value_parts:
+    for part in weight_parts:
         part.ring(1)
 
     @pl.loop(tiles // 2, tiles)
@@ -233,9 +226,7 @@
         norm_tile(i)
 
     wq_copy = load(query_hbm, wq)
-    for part in key_parts:
-        part.ring(2)
-    for part in value_parts:
+    for part in weight_parts:
         part.ring(2)
     for part in grad_parts:
         part.ring(1)
@@ -273,16 +264,14 @@
 
     for n in range(4):
         spread(dot(last_b, wq[:, pl.ds(512 * n, 512)]), 4 * n, q_all)
-    for part in key_parts:
+    for part in weight_parts:
         part.relay(2)
     for part in grad_parts:
         part.ring(2)
-    for part in key_parts:
+    for part in weight_parts:
         part.close()
-    for part in value_parts:
-        part.relay(2)
     wo_copy = load(out_hbm, wo)
-    for part in key_parts:
+    for part in weight_parts:
         finish(part.paired)
 
     def project(i, low):
@@ -290,19 +279,10 @@
         weight = kv[:, :, :, :, :, pl.ds(low, WIDTH)].reshape(WIDTH, WIDTH)
         joint[rows, pl.ds(low, WIDTH)] = dot(nb[rows, :], weight).astype(BF16)
 
-    @pl.loop(0, tiles // 2)
+    @pl.loop(0, tiles)
     def _(i):
         project(i, 0)
 
-    for part in value_parts:
-        part.close()
-
-    @pl.loop(tiles // 2, tiles)
-    def _(i):
-        project(i, 0)
-
-    for part in value_parts:
-        finish(part.paired)
     for part in grad_parts:
         part.relay(2)
 
@@ -525,20 +505,20 @@
     gain_sum[0] = gain_part
     gain_copies = [net.send(gain_sum.at[0], gain_pair, net.sibling)]
     halves(2)
+    input_grad(0)
     passed(0)
-    input_grad(0)
+    passed(1)
     finish(gain_copies)
     gain_copies = gain_round(0, gain_sum[0] + gain_pair[...])
-    passed(1)
     passed(2)
-    summed(0)
     input_grad(1)
     gain_copies = gain_round(1, gain_total(0, gain_copies))
+    summed(0)
     summed(1)
     summed(2)
-    summed_again(0)
     input_grad(2)
     gain_copies = gain_round(2, gain_total(1, gain_copies))
+    summed_again(0)
     summed_again(1)
     summed_again(2)
     input_grad(3)
@@ -614,8 +594,7 @@
             pltpu.SMEM((SLOTS,), jnp.int32),
             vmem(SLOTS, width, kind=F32),
             vmem(width),
-            vmem(SLOTS, WIDTH),
-            vmem(SLOTS, WIDTH),
+            vmem(SLOTS, 2 * WIDTH),
             pltpu.SemaphoreType.DMA((tokens // TILE,)),
         ],
         compiler_params=pltpu.CompilerParams(

time: 71.5 us -> 70.6 us (0.987)
  Pallas kernels: 68.2 us -> 67.3 us
    pallas_call x1, Pallas kernels: 68.2 us -> 67.3 us  [per_device(): pl.pallas_call(step_kernel, out_shape=(jax.ShapeDtypeStruct((tokens, widt...]
where the time goes in v5:
time: 70.6 us; the launch traced here: 70.5 us
  Pallas kernels  67.3 us (95%)
  local copies, waits for them, and re-layouts  2.54 us (4%)
    pallas_call x1, Pallas kernels, per_device(): pl.pallas_call(step_kernel, out_shape=(jax.ShapeDtypeStruct((tokens, widt...  67.3 us

profile of v5, /device:TPU:0, one launch (start us, length us, event | category | flops | bytes accessed | tf_op | source)
XLA Modules:
  0.0 70.5 jit_solution(5217322078960752109)
XLA Ops:
  0.6 67.3 %step.1 = (bf16[1024,1024]{1,0:T(8,128)(2,1)S(1)}, f32[16,2048]{1,0:T(8,128)S(1)}) custom-call(s32[1,8]{1,0:T(1,128)} %lengths_hbm.1, s32[8]{0:T(128)} %owner_hbm.1, bf16[128,8,1024]{2,1,0:T(8,128)(2,1)} %bitcast.2, f32[8,1024]{1,0:T(8,128)} %grad_hbm.1, bf16[1024]{0:T(1024)(128)(2,1)} %gain_hbm.1, bf16[1024,2048]{1,0:T(8,128)(2,1)} %query_hbm.1, ...), custom_call_target="tpu_custom_call" | custom-call | tf_op jit(solution)/shard_map/step/pallas_call | solution.py:547
  67.9 0.6 fusion
  68.6 0.6 slice.11
  69.2 1.3 %copy.14 = bf16[1024,1024]{1,0:T(8,128)(2,1)} copy(bf16[1024,1024]{1,0:T(8,128)(2,1)S(1)} %get-tuple-element.14) | data formatting | bytes 4194304
